TPU v7x, 32 devices: a whole 2x2x4 slice. The times are simulated.
32 devices in a mesh: dp: 16 (over z, x, core), tensor: 2 (over y).
Axes of the slice: x: 2, y: 2, z: 4, core: 2. Of those that a mesh axis runs over, the one named last changes fastest.
Arguments:
- tokens: bfloat16 [16, 736, 1152], P('dp', 'tensor'), may hold values from -6 to 6
- cotangent: bfloat16 [16, 736, 1152], P('dp', 'tensor'), may hold values from -6 to 6
- counts: int32 [16], P('dp'), may hold values from 638 to 729
- joint_weight: float32 [1152, 3, 1152], P('dp', None, 'tensor'), may hold values from -0.1875 to 0.1875
- joint_moment: float32 [1152, 3, 1152], P('dp', None, 'tensor'), may hold values from -0.0014648438 to 0.0014648438
- joint_square: float32 [1152, 3, 1152], P('dp', None, 'tensor'), may hold values from 4.53793e-09 to 3.630344e-08
- output_weight: float32 [1152, 1152], P('tensor', 'dp'), may hold values from -0.5 to 0.5
- output_moment: float32 [1152, 1152], P('tensor', 'dp'), may hold values from -0.0029296875 to 0.0029296875
- output_square: float32 [1152, 1152], P('tensor', 'dp'), may hold values from 1.815172e-08 to 1.4521376e-07
- expand_weight: float32 [1152, 4304], P('dp', 'tensor'), may hold values from -0.1875 to 0.1875
- expand_moment: float32 [1152, 4304], P('dp', 'tensor'), may hold values from -0.0029296875 to 0.0029296875
- expand_square: float32 [1152, 4304], P('dp', 'tensor'), may hold values from 1.815172e-08 to 1.4521376e-07
- reduce_weight: float32 [4304, 1152], P('tensor', 'dp'), may hold values from -0.09375 to 0.09375
- reduce_moment: float32 [4304, 1152], P('tensor', 'dp'), may hold values from -0.005859375 to 0.005859375
- reduce_square: float32 [4304, 1152], P('tensor', 'dp'), may hold values from 7.260688e-08 to 5.8085504e-07
- norm_gains: float32 [2, 1152], replicated, may hold values from 0.5 to 1.5
- gains_moment: float32 [2, 1152], replicated, may hold values from -0.009765625 to 0.009765625
- gains_square: float32 [2, 1152], replicated, may hold values from 2.0168576e-07 to 1.6134861e-06
- shifts: float32 [4, 1152], replicated, may hold values from -3 to 3
- shifts_moment: float32 [4, 1152], replicated, may hold values from -0.009765625 to 0.009765625
- shifts_square: float32 [4, 1152], replicated, may hold values from 2.0168576e-07 to 1.6134861e-06
- head_bias: float32 [2, 1152], P(None, 'tensor'), may hold values from -3 to 3
- head_moment: float32 [2, 1152], P(None, 'tensor'), may hold values from -0.0029296875 to 0.0029296875
- head_square: float32 [2, 1152], P(None, 'tensor'), may hold values from 1.815172e-08 to 1.4521376e-07
- hidden_bias: float32 [4304], P('tensor'), may hold values from -3 to 3
- hidden_moment: float32 [4304], P('tensor'), may hold values from -0.0029296875 to 0.0029296875
- hidden_square: float32 [4304], P('tensor'), may hold values from 1.815172e-08 to 1.4521376e-07
Outputs:
- layer_out: bfloat16 [16, 736, 1152], P('dp', 'tensor')
- input_grad: bfloat16 [16, 736, 1152], P('dp', 'tensor')
- grad_norm: float32 [], replicated
- joint_new: float32 [1152, 3, 1152], P('dp', None, 'tensor')
- joint_moment_new: float32 [1152, 3, 1152], P('dp', None, 'tensor')
- joint_square_new: float32 [1152, 3, 1152], P('dp', None, 'tensor')
- joint_copy: bfloat16 [1152, 3, 1152], P('dp', None, 'tensor')
- output_new: float32 [1152, 1152], P('tensor', 'dp')
- output_moment_new: float32 [1152, 1152], P('tensor', 'dp')
- output_square_new: float32 [1152, 1152], P('tensor', 'dp')
- output_copy: bfloat16 [1152, 1152], P('tensor', 'dp')
- expand_new: float32 [1152, 4304], P('dp', 'tensor')
- expand_moment_new: float32 [1152, 4304], P('dp', 'tensor')
- expand_square_new: float32 [1152, 4304], P('dp', 'tensor')
- expand_copy: bfloat16 [1152, 4304], P('dp', 'tensor')
- reduce_new: float32 [4304, 1152], P('tensor', 'dp')
- reduce_moment_new: float32 [4304, 1152], P('tensor', 'dp')
- reduce_square_new: float32 [4304, 1152], P('tensor', 'dp')
- reduce_copy: bfloat16 [4304, 1152], P('tensor', 'dp')
- gains_new: float32 [2, 1152], replicated
- gains_moment_new: float32 [2, 1152], replicated
- gains_square_new: float32 [2, 1152], replicated
- shifts_new: float32 [4, 1152], replicated
- shifts_moment_new: float32 [4, 1152], replicated
- shifts_square_new: float32 [4, 1152], replicated
- head_new: float32 [2, 1152], P(None, 'tensor')
- head_moment_new: float32 [2, 1152], P(None, 'tensor')
- head_square_new: float32 [2, 1152], P(None, 'tensor')
- hidden_new: float32 [4304], P('tensor')
- hidden_moment_new: float32 [4304], P('tensor')
- hidden_square_new: float32 [4304], P('tensor')
Inputs may be any that keep to these rules, and one draw needn't show every extreme that they name: `counts`: valid tokens of each image; key slots from there up to 736 are padding.
All inputs are finite; a program needn't handle non-finite values.
Results may differ from a plain program's by a relative error of at most 0.01.
Values may be sent and summed in bfloat16 or wider, within the bound.
A program may use at most 192 MiB of HBM per device.

v0:
```python
import jax
import jax.numpy as jnp
from jax import lax
from jax.sharding import PartitionSpec as P

HD = 72
STEP = 4
norm_eps = 1e-06
clip_limit = 1.0
matrix_rate = 0.03
vector_rate = 0.3
decay_rate = 0.1
adam_eps = 1e-08
mask_fill = -1e30


def layer_norm(values, gain, shift):
    center = jnp.mean(values, axis=-1, keepdims=True)
    centred = values - center
    spread = jnp.mean(centred * centred, axis=-1, keepdims=True)
    return centred * lax.rsqrt(spread + norm_eps) * gain + shift


def gelu_tanh(values):
    return jax.nn.gelu(values, approximate=True)


def whole_rows(part):
    return lax.all_gather(part, "tensor", axis=1, tiled=True)


def share_rows(full):
    return lax.psum_scatter(
        full.astype(jnp.bfloat16), "tensor", scatter_dimension=1, tiled=True
    ).astype(jnp.float32)


def scatter_sum(part, dim):
    return lax.psum_scatter(
        part.astype(jnp.bfloat16), "dp", scatter_dimension=dim, tiled=True
    ).astype(jnp.float32)


def split_heads(joint):
    length = joint.shape[0]
    heads_local = joint.shape[2] // HD
    query = joint[:, 0].reshape(length, heads_local, HD)
    keys = joint[:, 1].reshape(length, heads_local, HD)
    values = joint[:, 2].reshape(length, heads_local, HD)
    return (query, keys, values)


def masked_scores(query, keys, count):
    length = query.shape[0]
    scores = jnp.einsum("qhd,khd->hqk", query, keys, preferred_element_type=jnp.float32) * HD ** (
        -0.5
    )
    valid = jnp.arange(length, dtype=jnp.int32) < count
    return jnp.where(valid[None, None, :], scores, mask_fill)


def attend(joint, count):
    query, keys, values = split_heads(joint)
    scores = masked_scores(query, keys, count)
    top = jnp.max(scores, axis=-1, keepdims=True)
    total = jnp.sum(jnp.exp(scores - top), axis=-1, keepdims=True)
    logsum = top + jnp.log(total)
    probs = jnp.exp(scores - logsum)
    mixed = jnp.einsum(
        "hqk,khd->qhd", probs.astype(jnp.bfloat16), values, preferred_element_type=jnp.float32
    )
    return (mixed.reshape(joint.shape[0], joint.shape[2]).astype(jnp.bfloat16), logsum[:, :, 0])


def attend_back(joint, mixed_grad, logsum, count):
    query, keys, values = split_heads(joint)
    length = joint.shape[0]
    grad_heads = mixed_grad.reshape(length, joint.shape[2] // HD, HD)
    scores = masked_scores(query, keys, count)
    probs = jnp.exp(scores - logsum[:, :, None])
    value_grad = jnp.einsum(
        "hqk,qhd->khd", probs.astype(jnp.bfloat16), grad_heads, preferred_element_type=jnp.float32
    )
    prob_grad = jnp.einsum("qhd,khd->hqk", grad_heads, values, preferred_element_type=jnp.float32)
    inner = jnp.sum(probs * prob_grad, axis=-1, keepdims=True)
    score_grad = (probs * (prob_grad - inner)).astype(jnp.bfloat16)
    query_grad = jnp.einsum(
        "hqk,khd->qhd", score_grad, keys, preferred_element_type=jnp.float32
    ) * HD ** (-0.5)
    key_grad = jnp.einsum(
        "hqk,qhd->khd", score_grad, query, preferred_element_type=jnp.float32
    ) * HD ** (-0.5)
    stacked = jnp.stack([query_grad, key_grad, value_grad], axis=1)
    return stacked.reshape(length, 3, joint.shape[2]).astype(jnp.bfloat16)


def forward_pass(tokens, counts, weights, small):
    joint_w, expand_w, output_w, reduce_w = weights
    norm_gains, shifts, head_bias, hidden_bias = small
    rows = tokens.astype(jnp.float32)
    normed, first_back = jax.vjp(layer_norm, rows, norm_gains[0], shifts[0])
    normed_whole = whole_rows(normed.astype(jnp.bfloat16))
    joint = jnp.einsum("bsd,dch->bsch", normed_whole, joint_w, preferred_element_type=jnp.float32)
    bias = jnp.stack([head_bias[0], jnp.zeros_like(head_bias[0]), head_bias[1]])
    joint = (joint + bias).astype(jnp.bfloat16)
    mixed, logsum = lax.map(lambda pair: attend(pair[0], pair[1]), (joint, counts))
    branch = (
        share_rows(jnp.einsum("bsh,hd->bsd", mixed, output_w, preferred_element_type=jnp.float32))
        + shifts[2]
    )
    middle = rows + branch
    second, second_back = jax.vjp(layer_norm, middle, norm_gains[1], shifts[1])
    second_whole = whole_rows(second.astype(jnp.bfloat16))
    before = (
        jnp.einsum("bsd,df->bsf", second_whole, expand_w, preferred_element_type=jnp.float32)
        + hidden_bias
    )
    active, gelu_back = jax.vjp(gelu_tanh, before)
    active = active.astype(jnp.bfloat16)
    result = (
        share_rows(jnp.einsum("bsf,fd->bsd", active, reduce_w, preferred_element_type=jnp.float32))
        + shifts[3]
    )
    saved = (
        first_back,
        normed_whole,
        joint,
        mixed,
        logsum,
        second_back,
        second_whole,
        active,
        gelu_back,
    )
    return (middle + result, saved)


def adamw_step(weight, grad, moment, square, factor, rate, decay):
    clipped = grad * factor
    moment_new = 0.5 * moment + 0.5 * clipped
    square_new = 0.5 * square + 0.5 * clipped * clipped
    correct = 1.0 - 0.5**STEP
    update = moment_new / correct / (jnp.sqrt(square_new / correct) + adam_eps)
    return (weight - rate * (update + decay * weight), moment_new, square_new)


def squares(values):
    return jnp.sum(values * values)


def on_device(
    tokens,
    cotangent,
    counts,
    joint_weight,
    joint_moment,
    joint_square,
    output_weight,
    output_moment,
    output_square,
    expand_weight,
    expand_moment,
    expand_square,
    reduce_weight,
    reduce_moment,
    reduce_square,
    norm_gains,
    gains_moment,
    gains_square,
    shifts,
    shifts_moment,
    shifts_square,
    head_bias,
    head_moment,
    head_square,
    hidden_bias,
    hidden_moment,
    hidden_square,
):
    first_pair = (
        lax.all_gather(joint_weight.astype(jnp.bfloat16), "dp", axis=0, tiled=True),
        lax.all_gather(expand_weight.astype(jnp.bfloat16), "dp", axis=0, tiled=True),
    )
    second_pair = (
        lax.all_gather(output_weight.astype(jnp.bfloat16), "dp", axis=1, tiled=True),
        lax.all_gather(reduce_weight.astype(jnp.bfloat16), "dp", axis=1, tiled=True),
    )
    weights = (first_pair[0], first_pair[1], second_pair[0], second_pair[1])
    small = (norm_gains, shifts, head_bias, hidden_bias)
    layer_rows, saved = forward_pass(tokens, counts, weights, small)
    layer_out = layer_rows.astype(jnp.bfloat16)
    first_back, normed_whole, joint, mixed, logsum, second_back, second_whole, active, gelu_back = (
        saved
    )
    joint_w, expand_w, output_w, reduce_w = weights
    grad_rows = cotangent.astype(jnp.float32)
    grad_whole = whole_rows(cotangent)
    reduce_grad = jnp.einsum("bsf,bsd->fd", active, grad_whole, preferred_element_type=jnp.float32)
    active_grad = jnp.einsum(
        "bsd,fd->bsf", grad_whole, reduce_w, preferred_element_type=jnp.float32
    )
    before_grad = gelu_back(active_grad)[0].astype(jnp.bfloat16)
    expand_grad = jnp.einsum(
        "bsd,bsf->df", second_whole, before_grad, preferred_element_type=jnp.float32
    )
    hidden_grad = jnp.sum(before_grad, axis=(0, 1), dtype=jnp.float32)
    second_grad = share_rows(
        jnp.einsum("bsf,df->bsd", before_grad, expand_w, preferred_element_type=jnp.float32)
    )
    middle_part, gain_two, shift_two = second_back(second_grad)
    middle_grad = grad_rows + middle_part
    branch_grad = middle_grad.astype(jnp.bfloat16)
    branch_whole = whole_rows(branch_grad)
    output_grad = jnp.einsum("bsh,bsd->hd", mixed, branch_whole, preferred_element_type=jnp.float32)
    mixed_grad = jnp.einsum(
        "bsd,hd->bsh", branch_whole, output_w, preferred_element_type=jnp.float32
    ).astype(jnp.bfloat16)
    joint_grad = lax.map(
        lambda group: attend_back(group[0], group[1], group[2], group[3]),
        (joint, mixed_grad, logsum, counts),
    )
    joint_weight_grad = jnp.einsum(
        "bsd,bsch->dch", normed_whole, joint_grad, preferred_element_type=jnp.float32
    )
    head_grad = jnp.sum(joint_grad[:, :, 0::2], axis=(0, 1), dtype=jnp.float32)
    first_grad = share_rows(
        jnp.einsum("bsch,dch->bsd", joint_grad, joint_w, preferred_element_type=jnp.float32)
    )
    rows_part, gain_one, shift_one = first_back(first_grad)
    input_grad = (middle_grad + rows_part).astype(jnp.bfloat16)
    gain_grad = jnp.stack([gain_one, gain_two])
    shift_grad = jnp.stack(
        [
            shift_one,
            shift_two,
            jnp.sum(branch_grad, axis=(0, 1), dtype=jnp.float32),
            jnp.sum(grad_rows, axis=(0, 1)),
        ]
    )
    joint_sum, expand_sum = (scatter_sum(joint_weight_grad, 0), scatter_sum(expand_grad, 0))
    output_sum, reduce_sum = (scatter_sum(output_grad, 1), scatter_sum(reduce_grad, 1))
    gain_sum, shift_sum = lax.psum((gain_grad, shift_grad), ("dp", "tensor"))
    head_sum, hidden_sum = lax.psum((head_grad, hidden_grad), "dp")
    data_count = lax.axis_size("dp")
    split_count = lax.axis_size("tensor")
    owned = squares(joint_sum) + squares(expand_sum) + squares(output_sum) + squares(reduce_sum)
    shared = (squares(head_sum) + squares(hidden_sum)) / data_count
    everywhere = (squares(gain_sum) + squares(shift_sum)) / (data_count * split_count)
    grad_norm = jnp.sqrt(lax.psum(owned + shared + everywhere, ("dp", "tensor")))
    factor = clip_limit / jnp.maximum(grad_norm, clip_limit)
    joint_state = adamw_step(
        joint_weight, joint_sum, joint_moment, joint_square, factor, matrix_rate, decay_rate
    )
    output_state = adamw_step(
        output_weight, output_sum, output_moment, output_square, factor, matrix_rate, decay_rate
    )
    expand_state = adamw_step(
        expand_weight, expand_sum, expand_moment, expand_square, factor, matrix_rate, decay_rate
    )
    reduce_state = adamw_step(
        reduce_weight, reduce_sum, reduce_moment, reduce_square, factor, matrix_rate, decay_rate
    )
    gains_state = adamw_step(
        norm_gains, gain_sum, gains_moment, gains_square, factor, vector_rate, 0.0
    )
    shifts_state = adamw_step(
        shifts, shift_sum, shifts_moment, shifts_square, factor, vector_rate, 0.0
    )
    head_state = adamw_step(head_bias, head_sum, head_moment, head_square, factor, vector_rate, 0.0)
    hidden_state = adamw_step(
        hidden_bias, hidden_sum, hidden_moment, hidden_square, factor, vector_rate, 0.0
    )
    return (
        layer_out,
        input_grad,
        grad_norm,
        joint_state[0],
        joint_state[1],
        joint_state[2],
        joint_state[0].astype(jnp.bfloat16),
        output_state[0],
        output_state[1],
        output_state[2],
        output_state[0].astype(jnp.bfloat16),
        expand_state[0],
        expand_state[1],
        expand_state[2],
        expand_state[0].astype(jnp.bfloat16),
        reduce_state[0],
        reduce_state[1],
        reduce_state[2],
        reduce_state[0].astype(jnp.bfloat16),
        gains_state[0],
        gains_state[1],
        gains_state[2],
        shifts_state[0],
        shifts_state[1],
        shifts_state[2],
        head_state[0],
        head_state[1],
        head_state[2],
        hidden_state[0],
        hidden_state[1],
        hidden_state[2],
    )


def solution(mesh):
    in_specs = (
        P("dp", "tensor", None),
        P("dp", "tensor", None),
        P("dp"),
        P("dp", None, "tensor"),
        P("dp", None, "tensor"),
        P("dp", None, "tensor"),
        P("tensor", "dp"),
        P("tensor", "dp"),
        P("tensor", "dp"),
        P("dp", "tensor"),
        P("dp", "tensor"),
        P("dp", "tensor"),
        P("tensor", "dp"),
        P("tensor", "dp"),
        P("tensor", "dp"),
        P(),
        P(),
        P(),
        P(),
        P(),
        P(),
        P(None, "tensor"),
        P(None, "tensor"),
        P(None, "tensor"),
        P("tensor"),
        P("tensor"),
        P("tensor"),
    )
    out_specs = (
        P("dp", "tensor", None),
        P("dp", "tensor", None),
        P(),
        P("dp", None, "tensor"),
        P("dp", None, "tensor"),
        P("dp", None, "tensor"),
        P("dp", None, "tensor"),
        P("tensor", "dp"),
        P("tensor", "dp"),
        P("tensor", "dp"),
        P("tensor", "dp"),
        P("dp", "tensor"),
        P("dp", "tensor"),
        P("dp", "tensor"),
        P("dp", "tensor"),
        P("tensor", "dp"),
        P("tensor", "dp"),
        P("tensor", "dp"),
        P("tensor", "dp"),
        P(),
        P(),
        P(),
        P(),
        P(),
        P(),
        P(None, "tensor"),
        P(None, "tensor"),
        P(None, "tensor"),
        P("tensor"),
        P("tensor"),
        P("tensor"),
    )
    return jax.shard_map(
        on_device, mesh=mesh, in_specs=in_specs, out_specs=out_specs, check_vma=False
    )
```

profile of v0, /device:TPU:0, one launch (start us, length us, event | category | flops | bytes accessed | tf_op | source)
XLA Modules:
  0.0 853.5 jit_solution(2574007469518018370)
XLA Ops:
  17.5 29.0 %all-gather.9.cloned.1.call-done = bf16[1,736,1152]{2,1,0:T(8,128)(2,1)} async-done(((bf16[1,368,1152]{2,1,0:T(8,128)(2,1)}), bf16[1,736,1152]{2,1,0:T(8,128)(2,1)}) %all-gather.9.cloned.1.call-update) | async-done | bytes 1695760 | tf_op jit(solution)/shard_map/all_gather | solution.py:29
  46.5 54.5 %all-gather.11.cloned.1.call-done = bf16[1152,3,576]{2,0,1:T(8,128)(2,1)} async-done(((bf16[72,3,576]{2,0,1:T(8,128)(2,1)}), bf16[1152,3,576]{2,0,1:T(8,128)(2,1)}) %all-gather.11.cloned.1.call-update) | async-done | bytes 3981328 | tf_op jit(solution)/shard_map/all_gather | solution.py:181
  146.9 25.5 %reduce-scatter.17.cloned.1.call-done = bf16[1,368,1152]{2,1,0:T(8,128)(2,1)} async-done(((bf16[1,736,1152]{2,1,0:T(8,128)(2,1)}), bf16[1,368,1152]{2,1,0:T(8,128)(2,1)}) %reduce-scatter.17.cloned.1.call-update) | async-done | bytes 847888 | tf_op jit(solution)/shard_map/reduce_scatter | solution.py:33
  179.3 50.8 %all-gather.17.cloned.1.call-done = bf16[1152,2152]{1,0:T(8,128)(2,1)} async-done(((bf16[72,2152]{1,0:T(8,128)(2,1)}), bf16[1152,2152]{1,0:T(8,128)(2,1)}) %all-gather.17.cloned.1.call-update) | async-done | bytes 4958224 | tf_op jit(solution)/shard_map/all_gather | solution.py:182
  230.1 29.2 %all-gather.15.cloned.1.call-done = bf16[1,736,1152]{2,1,0:T(8,128)(2,1)} async-done(((bf16[1,368,1152]{2,1,0:T(8,128)(2,1)}), bf16[1,736,1152]{2,1,0:T(8,128)(2,1)}) %all-gather.15.cloned.1.call-update) | async-done | bytes 1695760 | tf_op jit(solution)/shard_map/all_gather | solution.py:29
  259.4 10.1 %fusion.38 = f32[736,2152]{1,0:T(8,128)} fusion(bf16[1152,2152]{1,0:T(8,128)(2,1)} %all-gather.17.cloned.1.call-done, bf16[1,736,1152]{2,1,0:T(8,128)(2,1)} %all-gather.15.cloned.1.call-done), kind=kOutput, calls=%fused_computation.72 | convolution fusion | flops 3649241088 | bytes 12989440 | tf_op jit(solution)/shard_map/bsd,df->bsf/dot_general | solution.py:115
  269.5 20.1 %all-gather.21.cloned.1.call-done = bf16[1,736,1152]{2,1,0:T(8,128)(2,1)} async-done(((bf16[1,368,1152]{2,1,0:T(8,128)(2,1)}), bf16[1,736,1152]{2,1,0:T(8,128)(2,1)}) %all-gather.21.cloned.1.call-update) | async-done | bytes 1695760 | tf_op jit(solution)/shard_map/all_gather | solution.py:29
  289.6 57.9 %all-gather.19.cloned.1.call-done = bf16[2152,1152]{0,1:T(8,128)(2,1)} async-done(((bf16[2152,72]{0,1:T(8,128)(2,1)}), bf16[2152,1152]{0,1:T(8,128)(2,1)}) %all-gather.19.cloned.1.call-update) | async-done | bytes 4958224 | tf_op jit(solution)/shard_map/all_gather | solution.py:186
  347.5 11.3 %convert_reduce_fusion = (f32[2152]{0:T(1024)S(1)}, bf16[736,2152]{1,0:T(8,128)(2,1)S(1)}) fusion(f32[736,2152]{1,0:T(8,128)} %fusion.38, f32[2152]{0:T(1024)S(1)} %copy-done.46, bf16[2152,1152]{0,1:T(8,128)(2,1)} %all-gather.19.cloned.1.call-done, bf16[1,736,1152]{2,1,0:T(8,128)(2,1)} %all-gather.21.cloned.1.call-done), kind=kOutput, calls=%fused_computation.18 | convolution fusion | flops 3685668096 | bytes 16174400 | tf_op jit(solution)/shard_map/bsd,fd->bsf/dot_general | solution.py:199
  368.9 11.1 %fusion.12 = bf16[1,736,1152]{2,1,0:T(8,128)(2,1)} fusion(bf16[2152,1152]{0,1:T(8,128)(2,1)} %all-gather.19.cloned.1.call-done, f32[736,2152]{1,0:T(8,128)} %fusion.38, f32[2152]{0:T(1024)S(1)} %copy-done.46), kind=kOutput, calls=%fused_computation.31 | convolution fusion | flops 3665927680 | bytes 12998048 | tf_op jit(solution)/shard_map/bsf,fd->bsd/dot_general | solution.py:121
  380.1 14.7 %reduce-scatter.21.cloned.1.call-done = bf16[1,368,1152]{2,1,0:T(8,128)(2,1)} async-done(((bf16[1,736,1152]{2,1,0:T(8,128)(2,1)}), bf16[1,368,1152]{2,1,0:T(8,128)(2,1)}) %reduce-scatter.21.cloned.1.call-update) | async-done | bytes 847888 | tf_op jit(solution)/shard_map/reduce_scatter | solution.py:33
  396.8 27.5 %reduce-scatter.19.cloned.1.call-done = bf16[1,368,1152]{2,1,0:T(8,128)(2,1)} async-done(((bf16[1,736,1152]{2,1,0:T(8,128)(2,1)}), bf16[1,368,1152]{2,1,0:T(8,128)(2,1)}) %reduce-scatter.19.cloned.1.call-update) | async-done | bytes 847888 | tf_op jit(solution)/shard_map/reduce_scatter | solution.py:33
  429.0 28.7 %all-gather.23.cloned.1.call-done = bf16[1,736,1152]{2,1,0:T(8,128)(2,1)} async-done(((bf16[1,368,1152]{2,1,0:T(8,128)(2,1)}), bf16[1,736,1152]{2,1,0:T(8,128)(2,1)}) %all-gather.23.cloned.1.call-update) | async-done | bytes 1695760 | tf_op jit(solution)/shard_map/all_gather | solution.py:29
  462.4 10.1 %convolution_convert_fusion = bf16[2152,1152]{0,1:T(8,128)(2,1)} fusion(bf16[1,736,1152]{2,1,0:T(8,128)(2,1)} %all-gather.21.cloned.1.call-done, f32[736,2152]{1,0:T(8,128)} %fusion.38, f32[2152]{0:T(1024)S(1)} %copy-done.46), kind=kOutput, calls=%fused_computation.6 | convolution fusion | flops 3667558912 | bytes 12998048 | tf_op jit(solution)/shard_map/bsf,bsd->fd/dot_general | solution.py:198
  491.4 13.2 %multiply_reduce_fusion = (f32[8,736]{1,0:T(8,128)S(1)}, f32[8,736,736]{1,2,0:T(8,128)}) fusion(f32[8,736,736]{1,2,0:T(8,128)} %get-tuple-element.122, f32[8,736]{1,0:T(8,128)S(1)} %log_add_fusion, pred[736]{0:T(1024)(128)(4,1)S(1)} %iota_compare_fusion, bf16[736,8,72]{0,2,1:T(8,128)(2,1)S(1)} %bitcast.108, bf16[736,8,72]{0,2,1:T(8,128)(2,1)S(1)} %bitcast.93), kind=kOutput, calls=%fused_computation.1 | convolution fusion | flops 645695744 | bytes 36412128 | tf_op jit(solution)/shard_map/while/body/eval_jaxpr/qhd,khd->hqk/dot_general | solution.py:84
  504.6 13.0 %multiply_convert_fusion = bf16[8,736,736]{1,2,0:T(8,128)(2,1)S(1)} fusion(f32[8,736,736]{1,2,0:T(8,128)} %get-tuple-element.124, f32[8,736,736]{1,2,0:T(8,128)} %get-tuple-element.122, f32[8,736]{1,0:T(8,128)S(1)} %get-tuple-element.123, f32[8,736]{1,0:T(8,128)S(1)} %log_add_fusion, pred[736]{0:T(1024)(128)(4,1)S(1)} %iota_compare_fusion), kind=kLoop, calls=%fused_computation | loop fusion | flops 26001408 | bytes 43383520 | tf_op jit(solution)/shard_map/while/body/eval_jaxpr/convert_element_type | solution.py:86
  535.2 18.2 %copy.70 = bf16[1152,3,576]{2,1,0:T(4,128)(2,1)} copy(bf16[1152,3,576]{2,0,1:T(8,128)(2,1)S(1)} %convolution_convert_fusion.2) | data formatting | bytes 7962624
  553.4 12.4 %reshape.392 = bf16[1152,1728]{1,0:T(8,128)(2,1)} reshape(bf16[1152,3,576]{2,1,0:T(4,128)(2,1)} %copy.70) | data formatting | bytes 7962624
  568.3 62.1 %all-reduce.4 = (f32[2,576]{1,0:T(2,128)S(1)}, f32[2152]{0:T(1024)S(1)}) all-reduce(f32[2,576]{1,0:T(2,128)S(1)} %convert_reduce_fusion.1, f32[2152]{0:T(1024)S(1)} %get-tuple-element.125), channel_id=1, replica_groups=mesh['dp'=16,'tensor'=2] {'dp'}, use_global_device_ids=true, to_apply=%region_24.25 | all-reduce | flops 3304 | bytes 26432 | tf_op jit(solution)/shard_map/psum | solution.py:243
  636.3 47.3 %reduce-scatter.27.cloned.1.call-done = bf16[72,2152]{1,0:T(8,128)(2,1)} async-done(((bf16[1152,2152]{1,0:T(8,128)(2,1)}), bf16[72,2152]{1,0:T(8,128)(2,1)}) %reduce-scatter.27.cloned.1.call-update) | async-done | bytes 309904
  685.4 26.8 %reduce-scatter.23.cloned.1.call-done = bf16[1,368,1152]{2,1,0:T(8,128)(2,1)} async-done(((bf16[1,736,1152]{2,1,0:T(8,128)(2,1)}), bf16[1,368,1152]{2,1,0:T(8,128)(2,1)}) %reduce-scatter.23.cloned.1.call-update) | async-done | bytes 847888 | tf_op jit(solution)/shard_map/reduce_scatter | solution.py:33
  717.9 40.8 %all-reduce.3 = (f32[2,1152]{1,0:T(2,128)S(1)}, f32[4,1152]{1,0:T(4,128)S(1)}) all-reduce(f32[2,1152]{1,0:T(2,128)S(1)} %pad_maximum_fusion.6, f32[4,1152]{1,0:T(4,128)S(1)} %pad_maximum_fusion.4), channel_id=1, replica_groups=mesh['dp'=16,'tensor'=2] {'dp','tensor'}, use_global_device_ids=true, to_apply=%region_31.32 | all-reduce | flops 6912 | bytes 55296 | tf_op jit(solution)/shard_map/psum | solution.py:242
  761.3 27.2 %reduce-scatter.25.cloned.1.call-done = bf16[72,1728]{1,0:T(8,128)(2,1)} async-done(((bf16[1152,1728]{1,0:T(8,128)(2,1)}), bf16[72,1728]{1,0:T(8,128)(2,1)}) %reduce-scatter.25.cloned.1.call-update) | async-done | bytes 248848
  793.0 39.4 %psum.39 = f32[]{:T(128)} all-reduce(f32[]{:T(128)S(6)} %add.313), channel_id=1, replica_groups=mesh['dp'=16,'tensor'=2] {'dp','tensor'}, use_global_device_ids=true, to_apply=%region_39.40 | all-reduce | flops 1 | bytes 8 | tf_op jit(solution)/shard_map/psum | solution.py:249
  (210 shorter events, 149.7 us)
Async XLA Ops:
  7.2 39.3 %all-gather.9.cloned.1.call-start = ((), (), s32[]{:S(2)}) async-start(), calls=%async_computation.8 | async-start | bytes 2543616 | tf_op jit(solution)/shard_map/all_gather | solution.py:29
  15.0 86.0 %all-gather.11.cloned.1.call-start = ((), (), s32[]{:S(2)}) async-start(), calls=%async_computation.9 | async-start | bytes 4700160 | tf_op jit(solution)/shard_map/all_gather | solution.py:181
  15.9 125.8 %all-gather.13.cloned.1.call-start = ((), (), s32[]{:S(2)}) async-start(), calls=%async_computation.10 | async-start | bytes 1566720 | tf_op jit(solution)/shard_map/all_gather | solution.py:185
  16.6 155.8 %reduce-scatter.17.cloned.1.call-start = ((), (), s32[]{:S(2)}) async-start(), calls=%async_computation.11 | async-start | bytes 2543616 | tf_op jit(solution)/shard_map/reduce_scatter | solution.py:33
  146.0 84.2 %all-gather.17.cloned.1.call-start = ((), (), s32[]{:S(2)}) async-start(), calls=%async_computation.13 | async-start | bytes 5326848 | tf_op jit(solution)/shard_map/all_gather | solution.py:182
  146.8 112.6 %all-gather.15.cloned.1.call-start = ((), (), s32[]{:S(2)}) async-start(), calls=%async_computation.12 | async-start | bytes 2543616 | tf_op jit(solution)/shard_map/all_gather | solution.py:29
  177.2 112.5 %all-gather.21.cloned.1.call-start = ((), (), s32[]{:S(2)}) async-start(), calls=%async_computation.16 | async-start | bytes 2543616 | tf_op jit(solution)/shard_map/all_gather | solution.py:29
  177.9 169.6 %all-gather.19.cloned.1.call-start = ((), (), s32[]{:S(2)}) async-start(), calls=%async_computation.14 | async-start | bytes 5326848 | tf_op jit(solution)/shard_map/all_gather | solution.py:186
  178.7 168.8 %copy-start.46 = (f32[2152]{0:T(1024)S(1)}, f32[2152]{0:T(1024)}, u32[]{:S(2)}) copy-start(f32[2152]{0:T(1024)} %param.51) | copy-start | bytes 25828
  178.8 216.0 %reduce-scatter.21.cloned.1.call-start = ((), (), s32[]{:S(2)}) async-start(), calls=%async_computation.17 | async-start | bytes 2543616 | tf_op jit(solution)/shard_map/reduce_scatter | solution.py:33
  368.7 55.7 %reduce-scatter.19.cloned.1.call-start = ((), (), s32[]{:S(2)}) async-start(), calls=%async_computation.15 | async-start | bytes 2543616 | tf_op jit(solution)/shard_map/reduce_scatter | solution.py:33
  380.0 77.7 %all-gather.23.cloned.1.call-start = ((), (), s32[]{:S(2)}) async-start(), calls=%async_computation.18 | async-start | bytes 2543616 | tf_op jit(solution)/shard_map/all_gather | solution.py:29
  428.9 204.0 %reduce-scatter.29.cloned.1.call-start = ((), (), s32[]{:S(2)}) async-start(), calls=%async_computation.22 | async-start | bytes 1566720
  462.2 172.3 %reduce-scatter.31.cloned.1.call-start = ((), (), s32[]{:S(2)}) async-start(), calls=%async_computation.23 | async-start | bytes 5326848
  472.5 211.1 %reduce-scatter.27.cloned.1.call-start = ((), (), s32[]{:S(2)}) async-start(), calls=%async_computation.21 | async-start | bytes 5326848
  481.7 230.4 %reduce-scatter.23.cloned.1.call-start = ((), (), s32[]{:S(2)}) async-start(), calls=%async_computation.19 | async-start | bytes 2543616 | tf_op jit(solution)/shard_map/reduce_scatter | solution.py:33
  528.6 259.9 %reduce-scatter.25.cloned.1.call-start = ((), (), s32[]{:S(2)}) async-start(), calls=%async_computation.20 | async-start | bytes 4386816
  565.8 146.3 %copy-start.31 = (f32[1152]{0:T(1024)S(1)}, f32[1152]{0:T(1024)}, u32[]{:S(2)}) copy-start(f32[1152]{0:T(1024)} %copy-done.30) | copy-start | bytes 13828
  565.9 146.3 %copy-start.36 = (f32[368]{0:T(512)S(1)}, f32[368]{0:T(512)}, u32[]{:S(2)}) copy-start(f32[368]{0:T(512)} %copy-done.35) | copy-start | bytes 4420
  567.9 146.0 %copy-start.45 = (f32[368]{0:T(512)S(1)}, f32[368]{0:T(512)}, u32[]{:S(2)}) copy-start(f32[368]{0:T(512)} %copy-done.44) | copy-start | bytes 4420
  568.0 146.0 %copy-start.39 = (f32[368]{0:T(512)S(1)}, f32[368]{0:T(512)}, u32[]{:S(2)}) copy-start(f32[368]{0:T(512)} %copy-done.38) | copy-start | bytes 4420
  568.0 148.0 %copy-start.10 = (bf16[1,368,1152]{2,1,0:T(8,128)(2,1)S(1)}, bf16[1,368,1152]{2,1,0:T(8,128)(2,1)}, u32[]{:S(2)}) copy-start(bf16[1,368,1152]{2,1,0:T(8,128)(2,1)} %param.28) | copy-start | bytes 2543620
  716.0 121.2 %copy-start.34 = (f32[4,1152]{1,0:T(4,128)S(1)}, f32[4,1152]{1,0:T(4,128)}, u32[]{:S(2)}) copy-start(f32[4,1152]{1,0:T(4,128)} %param.45) | copy-start | bytes 55300
  716.1 121.2 %copy-start.42 = (f32[4,1152]{1,0:T(4,128)S(1)}, f32[4,1152]{1,0:T(4,128)}, u32[]{:S(2)}) copy-start(f32[4,1152]{1,0:T(4,128)} %param.46) | copy-start | bytes 55300
  (42 other events, 1192.7 us)
Sparse Core Ops, SparseCore 0:
  15.2 31.2 all-gather.8
  49.3 51.7 all-gather.10
  103.8 37.8 all-gather.12
  146.1 26.2 reduce-scatter.16
  175.2 54.8 all-gather.16
  232.2 27.1 all-gather.14
  261.0 28.5 all-gather.20
  292.6 54.9 all-gather.18
  368.8 25.9 reduce-scatter.20
  396.9 27.4 reduce-scatter.18
  429.1 28.5 all-gather.22
  462.3 58.7 reduce-scatter.28
  525.6 77.2 reduce-scatter.30
  606.7 76.8 reduce-scatter.26
  685.8 26.2 reduce-scatter.22
  715.9 72.6 reduce-scatter.24
where the time goes:
time: 859 us; the launch traced here: 853 us
  waiting for transfers between devices  442 us (51%)
  blocking collectives  142 us (17%)
  matrix products  124 us (14%)
  other arithmetic  79.5 us (9%)
  local copies, waits for them, and re-layouts  40.6 us (5%)
  between operations  22.6 us (3%)
    all_gather x4, waiting for transfers between devices, whole_rows(): return lax.all_gather(part, 'tensor', axis=1, tiled=True)  107 us
    reduce_scatter x4, waiting for transfers between devices, share_rows(): lax.psum_scatter(full.astype(jnp.bfloat16), 'tensor', scatter_dimension=1...  94.5 us
    unnamed x20, waiting for transfers between devices  75.5 us
    psum x1, blocking collectives, on_device(): head_sum, hidden_sum = lax.psum((head_grad, hidden_grad), 'dp')  62.1 us
    all_gather x1, waiting for transfers between devices, on_device(): lax.all_gather(reduce_weight.astype(jnp.bfloat16), 'dp', axis=1, tiled=True)  57.9 us
    all_gather x1, waiting for transfers between devices, on_device(): lax.all_gather(joint_weight.astype(jnp.bfloat16), 'dp', axis=0, tiled=True)  54.5 us
    all_gather x1, waiting for transfers between devices, on_device(): lax.all_gather(expand_weight.astype(jnp.bfloat16), 'dp', axis=0, tiled=True)  50.8 us
    psum x1, blocking collectives, on_device(): gain_sum, shift_sum = lax.psum((gain_grad, shift_grad), ('dp', 'tensor'))  40.8 us
  transfers between devices with their start and end apart: 16, of which 14 were waited for; matrix products, arithmetic and copies ran while one was open for 22% of the time, Pallas kernels for 0%

commit v1 on v0

--- a/solution.py
+++ b/solution.py
@@ -246,7 +246,9 @@
     owned = squares(joint_sum) + squares(expand_sum) + squares(output_sum) + squares(reduce_sum)
     shared = (squares(head_sum) + squares(hidden_sum)) / data_count
     everywhere = (squares(gain_sum) + squares(shift_sum)) / (data_count * split_count)
-    grad_norm = jnp.sqrt(lax.psum(owned + shared + everywhere, ("dp", "tensor")))
+    grad_norm = jnp.sqrt(
+        jnp.sum(lax.all_gather(owned + shared + everywhere, ("dp", "tensor")), axis=0)
+    )
     factor = clip_limit / jnp.maximum(grad_norm, clip_limit)
     joint_state = adamw_step(
         joint_weight, joint_sum, joint_moment, joint_square, factor, matrix_rate, decay_rate

time: 859 us -> 860 us (level)
    psum x1 -> x0, blocking collectives: 39.4 us -> none  [on_device(): lax.psum(owned + shared + everywhere, ('dp', 'tensor'))]
    unnamed x0 -> x1, blocking collectives: none -> 39.4 us
    unnamed x103 -> x105, local copies, waits for them, and re-layouts: 38.6 us -> 38.7 us
where the time goes in v1:
time: 860 us; the launch traced here: 854 us
  waiting for transfers between devices  442 us (51%)
  blocking collectives  142 us (17%)
  matrix products  124 us (14%)
  other arithmetic  80.1 us (9%)
  local copies, waits for them, and re-layouts  40.7 us (5%)
  between operations  22.7 us (3%)
    all_gather x4, waiting for transfers between devices, whole_rows(): return lax.all_gather(part, 'tensor', axis=1, tiled=True)  107 us
    reduce_scatter x4, waiting for transfers between devices, share_rows(): lax.psum_scatter(full.astype(jnp.bfloat16), 'tensor', scatter_dimension=1...  94.6 us
    unnamed x20, waiting for transfers between devices  75.5 us
    psum x1, blocking collectives, on_device(): head_sum, hidden_sum = lax.psum((head_grad, hidden_grad), 'dp')  62.1 us
    all_gather x1, waiting for transfers between devices, on_device(): lax.all_gather(reduce_weight.astype(jnp.bfloat16), 'dp', axis=1, tiled=True)  57.9 us
    all_gather x1, waiting for transfers between devices, on_device(): lax.all_gather(joint_weight.astype(jnp.bfloat16), 'dp', axis=0, tiled=True)  54.5 us
    all_gather x1, waiting for transfers between devices, on_device(): lax.all_gather(expand_weight.astype(jnp.bfloat16), 'dp', axis=0, tiled=True)  50.8 us
    psum x1, blocking collectives, on_device(): gain_sum, shift_sum = lax.psum((gain_grad, shift_grad), ('dp', 'tensor'))  40.8 us
  transfers between devices with their start and end apart: 16, of which 14 were waited for; matrix products, arithmetic and copies ran while one was open for 22% of the time, Pallas kernels for 0%

profile of v1, /device:TPU:0, one launch (start us, length us, event | category | flops | bytes accessed | tf_op | source)
XLA Modules:
  0.0 854.2 jit_solution(17201791039122829181)
XLA Ops:
  17.5 29.0 %all-gather.9.cloned.1.call-done = bf16[1,736,1152]{2,1,0:T(8,128)(2,1)} async-done(((bf16[1,368,1152]{2,1,0:T(8,128)(2,1)}), bf16[1,736,1152]{2,1,0:T(8,128)(2,1)}) %all-gather.9.cloned.1.call-update) | async-done | bytes 1695760 | tf_op jit(solution)/shard_map/all_gather | solution.py:29
  46.5 54.5 %all-gather.11.cloned.1.call-done = bf16[1152,3,576]{2,0,1:T(8,128)(2,1)} async-done(((bf16[72,3,576]{2,0,1:T(8,128)(2,1)}), bf16[1152,3,576]{2,0,1:T(8,128)(2,1)}) %all-gather.11.cloned.1.call-update) | async-done | bytes 3981328 | tf_op jit(solution)/shard_map/all_gather | solution.py:181
  146.8 25.5 %reduce-scatter.17.cloned.1.call-done = bf16[1,368,1152]{2,1,0:T(8,128)(2,1)} async-done(((bf16[1,736,1152]{2,1,0:T(8,128)(2,1)}), bf16[1,368,1152]{2,1,0:T(8,128)(2,1)}) %reduce-scatter.17.cloned.1.call-update) | async-done | bytes 847888 | tf_op jit(solution)/shard_map/reduce_scatter | solution.py:33
  179.3 50.8 %all-gather.17.cloned.1.call-done = bf16[1152,2152]{1,0:T(8,128)(2,1)} async-done(((bf16[72,2152]{1,0:T(8,128)(2,1)}), bf16[1152,2152]{1,0:T(8,128)(2,1)}) %all-gather.17.cloned.1.call-update) | async-done | bytes 4958224 | tf_op jit(solution)/shard_map/all_gather | solution.py:182
  230.1 29.2 %all-gather.15.cloned.1.call-done = bf16[1,736,1152]{2,1,0:T(8,128)(2,1)} async-done(((bf16[1,368,1152]{2,1,0:T(8,128)(2,1)}), bf16[1,736,1152]{2,1,0:T(8,128)(2,1)}) %all-gather.15.cloned.1.call-update) | async-done | bytes 1695760 | tf_op jit(solution)/shard_map/all_gather | solution.py:29
  259.3 10.1 %fusion.38 = f32[736,2152]{1,0:T(8,128)} fusion(bf16[1152,2152]{1,0:T(8,128)(2,1)} %all-gather.17.cloned.1.call-done, bf16[1,736,1152]{2,1,0:T(8,128)(2,1)} %all-gather.15.cloned.1.call-done), kind=kOutput, calls=%fused_computation.72 | convolution fusion | flops 3649241088 | bytes 12989440 | tf_op jit(solution)/shard_map/bsd,df->bsf/dot_general | solution.py:115
  269.5 20.1 %all-gather.21.cloned.1.call-done = bf16[1,736,1152]{2,1,0:T(8,128)(2,1)} async-done(((bf16[1,368,1152]{2,1,0:T(8,128)(2,1)}), bf16[1,736,1152]{2,1,0:T(8,128)(2,1)}) %all-gather.21.cloned.1.call-update) | async-done | bytes 1695760 | tf_op jit(solution)/shard_map/all_gather | solution.py:29
  289.6 57.9 %all-gather.19.cloned.1.call-done = bf16[2152,1152]{0,1:T(8,128)(2,1)} async-done(((bf16[2152,72]{0,1:T(8,128)(2,1)}), bf16[2152,1152]{0,1:T(8,128)(2,1)}) %all-gather.19.cloned.1.call-update) | async-done | bytes 4958224 | tf_op jit(solution)/shard_map/all_gather | solution.py:186
  347.5 11.3 %convert_reduce_fusion = (f32[2152]{0:T(1024)S(1)}, bf16[736,2152]{1,0:T(8,128)(2,1)S(1)}) fusion(f32[736,2152]{1,0:T(8,128)} %fusion.38, f32[2152]{0:T(1024)S(1)} %copy-done.46, bf16[2152,1152]{0,1:T(8,128)(2,1)} %all-gather.19.cloned.1.call-done, bf16[1,736,1152]{2,1,0:T(8,128)(2,1)} %all-gather.21.cloned.1.call-done), kind=kOutput, calls=%fused_computation.18 | convolution fusion | flops 3685668096 | bytes 16174400 | tf_op jit(solution)/shard_map/bsd,fd->bsf/dot_general | solution.py:199
  368.9 11.1 %fusion.12 = bf16[1,736,1152]{2,1,0:T(8,128)(2,1)} fusion(bf16[2152,1152]{0,1:T(8,128)(2,1)} %all-gather.19.cloned.1.call-done, f32[736,2152]{1,0:T(8,128)} %fusion.38, f32[2152]{0:T(1024)S(1)} %copy-done.46), kind=kOutput, calls=%fused_computation.31 | convolution fusion | flops 3665927680 | bytes 12998048 | tf_op jit(solution)/shard_map/bsf,fd->bsd/dot_general | solution.py:121
  380.0 14.7 %reduce-scatter.21.cloned.1.call-done = bf16[1,368,1152]{2,1,0:T(8,128)(2,1)} async-done(((bf16[1,736,1152]{2,1,0:T(8,128)(2,1)}), bf16[1,368,1152]{2,1,0:T(8,128)(2,1)}) %reduce-scatter.21.cloned.1.call-update) | async-done | bytes 847888 | tf_op jit(solution)/shard_map/reduce_scatter | solution.py:33
  396.8 27.5 %reduce-scatter.19.cloned.1.call-done = bf16[1,368,1152]{2,1,0:T(8,128)(2,1)} async-done(((bf16[1,736,1152]{2,1,0:T(8,128)(2,1)}), bf16[1,368,1152]{2,1,0:T(8,128)(2,1)}) %reduce-scatter.19.cloned.1.call-update) | async-done | bytes 847888 | tf_op jit(solution)/shard_map/reduce_scatter | solution.py:33
  428.9 28.7 %all-gather.23.cloned.1.call-done = bf16[1,736,1152]{2,1,0:T(8,128)(2,1)} async-done(((bf16[1,368,1152]{2,1,0:T(8,128)(2,1)}), bf16[1,736,1152]{2,1,0:T(8,128)(2,1)}) %all-gather.23.cloned.1.call-update) | async-done | bytes 1695760 | tf_op jit(solution)/shard_map/all_gather | solution.py:29
  462.4 10.1 %convolution_convert_fusion = bf16[2152,1152]{0,1:T(8,128)(2,1)} fusion(bf16[1,736,1152]{2,1,0:T(8,128)(2,1)} %all-gather.21.cloned.1.call-done, f32[736,2152]{1,0:T(8,128)} %fusion.38, f32[2152]{0:T(1024)S(1)} %copy-done.46), kind=kOutput, calls=%fused_computation.6 | convolution fusion | flops 3667558912 | bytes 12998048 | tf_op jit(solution)/shard_map/bsf,bsd->fd/dot_general | solution.py:198
  491.4 13.2 %multiply_reduce_fusion = (f32[8,736]{1,0:T(8,128)S(1)}, f32[8,736,736]{1,2,0:T(8,128)}) fusion(f32[8,736,736]{1,2,0:T(8,128)} %get-tuple-element.122, f32[8,736]{1,0:T(8,128)S(1)} %log_add_fusion, pred[736]{0:T(1024)(128)(4,1)S(1)} %iota_compare_fusion, bf16[736,8,72]{0,2,1:T(8,128)(2,1)S(1)} %bitcast.109, bf16[736,8,72]{0,2,1:T(8,128)(2,1)S(1)} %bitcast.94), kind=kOutput, calls=%fused_computation.1 | convolution fusion | flops 645695744 | bytes 36412128 | tf_op jit(solution)/shard_map/while/body/eval_jaxpr/qhd,khd->hqk/dot_general | solution.py:84
  504.6 13.0 %multiply_convert_fusion = bf16[8,736,736]{1,2,0:T(8,128)(2,1)S(1)} fusion(f32[8,736,736]{1,2,0:T(8,128)} %get-tuple-element.124, f32[8,736,736]{1,2,0:T(8,128)} %get-tuple-element.122, f32[8,736]{1,0:T(8,128)S(1)} %get-tuple-element.123, f32[8,736]{1,0:T(8,128)S(1)} %log_add_fusion, pred[736]{0:T(1024)(128)(4,1)S(1)} %iota_compare_fusion), kind=kLoop, calls=%fused_computation | loop fusion | flops 26001408 | bytes 43383520 | tf_op jit(solution)/shard_map/while/body/eval_jaxpr/convert_element_type | solution.py:86
  535.2 18.2 %copy.70 = bf16[1152,3,576]{2,1,0:T(4,128)(2,1)} copy(bf16[1152,3,576]{2,0,1:T(8,128)(2,1)S(1)} %convolution_convert_fusion.2) | data formatting | bytes 7962624
  553.4 12.3 %reshape.394 = bf16[1152,1728]{1,0:T(8,128)(2,1)} reshape(bf16[1152,3,576]{2,1,0:T(4,128)(2,1)} %copy.70) | data formatting | bytes 7962624
  568.3 62.1 %all-reduce.5 = (f32[2,576]{1,0:T(2,128)S(1)}, f32[2152]{0:T(1024)S(1)}) all-reduce(f32[2,576]{1,0:T(2,128)S(1)} %convert_reduce_fusion.1, f32[2152]{0:T(1024)S(1)} %get-tuple-element.125), channel_id=1, replica_groups=mesh['dp'=16,'tensor'=2] {'dp'}, use_global_device_ids=true, to_apply=%region_24.25 | all-reduce | flops 3304 | bytes 26432 | tf_op jit(solution)/shard_map/psum | solution.py:243
  636.3 47.3 %reduce-scatter.27.cloned.1.call-done = bf16[72,2152]{1,0:T(8,128)(2,1)} async-done(((bf16[1152,2152]{1,0:T(8,128)(2,1)}), bf16[72,2152]{1,0:T(8,128)(2,1)}) %reduce-scatter.27.cloned.1.call-update) | async-done | bytes 309904
  685.4 26.8 %reduce-scatter.23.cloned.1.call-done = bf16[1,368,1152]{2,1,0:T(8,128)(2,1)} async-done(((bf16[1,736,1152]{2,1,0:T(8,128)(2,1)}), bf16[1,368,1152]{2,1,0:T(8,128)(2,1)}) %reduce-scatter.23.cloned.1.call-update) | async-done | bytes 847888 | tf_op jit(solution)/shard_map/reduce_scatter | solution.py:33
  718.0 40.8 %all-reduce.4 = (f32[2,1152]{1,0:T(2,128)S(1)}, f32[4,1152]{1,0:T(4,128)S(1)}) all-reduce(f32[2,1152]{1,0:T(2,128)S(1)} %pad_maximum_fusion.6, f32[4,1152]{1,0:T(4,128)S(1)} %pad_maximum_fusion.4), channel_id=1, replica_groups=mesh['dp'=16,'tensor'=2] {'dp','tensor'}, use_global_device_ids=true, to_apply=%region_31.32 | all-reduce | flops 6912 | bytes 55296 | tf_op jit(solution)/shard_map/psum | solution.py:242
  761.4 27.2 %reduce-scatter.25.cloned.1.call-done = bf16[72,1728]{1,0:T(8,128)(2,1)} async-done(((bf16[1152,1728]{1,0:T(8,128)(2,1)}), bf16[72,1728]{1,0:T(8,128)(2,1)}) %reduce-scatter.25.cloned.1.call-update) | async-done | bytes 248848
  793.2 39.4 %all-reduce = f32[32]{0:T(128)S(1)} all-reduce(f32[32]{0:T(128)S(1)} %dynamic-update-slice), channel_id=1, replica_groups=mesh['dp'=16,'tensor'=2] {'dp','tensor'}, use_global_device_ids=true, to_apply=%add | all-reduce | flops 32 | bytes 256
  (213 shorter events, 150.5 us)
Async XLA Ops:
  7.2 39.3 %all-gather.9.cloned.1.call-start = ((), (), s32[]{:S(2)}) async-start(), calls=%async_computation.8 | async-start | bytes 2543616 | tf_op jit(solution)/shard_map/all_gather | solution.py:29
  15.0 86.0 %all-gather.11.cloned.1.call-start = ((), (), s32[]{:S(2)}) async-start(), calls=%async_computation.9 | async-start | bytes 4700160 | tf_op jit(solution)/shard_map/all_gather | solution.py:181
  15.9 125.8 %all-gather.13.cloned.1.call-start = ((), (), s32[]{:S(2)}) async-start(), calls=%async_computation.10 | async-start | bytes 1566720 | tf_op jit(solution)/shard_map/all_gather | solution.py:185
  16.6 155.8 %reduce-scatter.17.cloned.1.call-start = ((), (), s32[]{:S(2)}) async-start(), calls=%async_computation.11 | async-start | bytes 2543616 | tf_op jit(solution)/shard_map/reduce_scatter | solution.py:33
  146.0 84.2 %all-gather.17.cloned.1.call-start = ((), (), s32[]{:S(2)}) async-start(), calls=%async_computation.13 | async-start | bytes 5326848 | tf_op jit(solution)/shard_map/all_gather | solution.py:182
  146.8 112.6 %all-gather.15.cloned.1.call-start = ((), (), s32[]{:S(2)}) async-start(), calls=%async_computation.12 | async-start | bytes 2543616 | tf_op jit(solution)/shard_map/all_gather | solution.py:29
  177.1 112.5 %all-gather.21.cloned.1.call-start = ((), (), s32[]{:S(2)}) async-start(), calls=%async_computation.16 | async-start | bytes 2543616 | tf_op jit(solution)/shard_map/all_gather | solution.py:29
  177.9 169.6 %all-gather.19.cloned.1.call-start = ((), (), s32[]{:S(2)}) async-start(), calls=%async_computation.14 | async-start | bytes 5326848 | tf_op jit(solution)/shard_map/all_gather | solution.py:186
  178.7 168.8 %copy-start.46 = (f32[2152]{0:T(1024)S(1)}, f32[2152]{0:T(1024)}, u32[]{:S(2)}) copy-start(f32[2152]{0:T(1024)} %param.51) | copy-start | bytes 25828
  178.7 216.0 %reduce-scatter.21.cloned.1.call-start = ((), (), s32[]{:S(2)}) async-start(), calls=%async_computation.17 | async-start | bytes 2543616 | tf_op jit(solution)/shard_map/reduce_scatter | solution.py:33
  368.6 55.7 %reduce-scatter.19.cloned.1.call-start = ((), (), s32[]{:S(2)}) async-start(), calls=%async_computation.15 | async-start | bytes 2543616 | tf_op jit(solution)/shard_map/reduce_scatter | solution.py:33
  380.0 77.7 %all-gather.23.cloned.1.call-start = ((), (), s32[]{:S(2)}) async-start(), calls=%async_computation.18 | async-start | bytes 2543616 | tf_op jit(solution)/shard_map/all_gather | solution.py:29
  428.9 204.0 %reduce-scatter.29.cloned.1.call-start = ((), (), s32[]{:S(2)}) async-start(), calls=%async_computation.22 | async-start | bytes 1566720
  462.1 172.3 %reduce-scatter.31.cloned.1.call-start = ((), (), s32[]{:S(2)}) async-start(), calls=%async_computation.23 | async-start | bytes 5326848
  472.5 211.1 %reduce-scatter.27.cloned.1.call-start = ((), (), s32[]{:S(2)}) async-start(), calls=%async_computation.21 | async-start | bytes 5326848
  481.6 230.5 %reduce-scatter.23.cloned.1.call-start = ((), (), s32[]{:S(2)}) async-start(), calls=%async_computation.19 | async-start | bytes 2543616 | tf_op jit(solution)/shard_map/reduce_scatter | solution.py:33
  528.6 260.0 %reduce-scatter.25.cloned.1.call-start = ((), (), s32[]{:S(2)}) async-start(), calls=%async_computation.20 | async-start | bytes 4386816
  565.8 146.3 %copy-start.31 = (f32[1152]{0:T(1024)S(1)}, f32[1152]{0:T(1024)}, u32[]{:S(2)}) copy-start(f32[1152]{0:T(1024)} %copy-done.30) | copy-start | bytes 13828
  565.9 146.3 %copy-start.36 = (f32[368]{0:T(512)S(1)}, f32[368]{0:T(512)}, u32[]{:S(2)}) copy-start(f32[368]{0:T(512)} %copy-done.35) | copy-start | bytes 4420
  567.9 146.0 %copy-start.45 = (f32[368]{0:T(512)S(1)}, f32[368]{0:T(512)}, u32[]{:S(2)}) copy-start(f32[368]{0:T(512)} %copy-done.44) | copy-start | bytes 4420
  567.9 146.0 %copy-start.39 = (f32[368]{0:T(512)S(1)}, f32[368]{0:T(512)}, u32[]{:S(2)}) copy-start(f32[368]{0:T(512)} %copy-done.38) | copy-start | bytes 4420
  568.0 148.1 %copy-start.10 = (bf16[1,368,1152]{2,1,0:T(8,128)(2,1)S(1)}, bf16[1,368,1152]{2,1,0:T(8,128)(2,1)}, u32[]{:S(2)}) copy-start(bf16[1,368,1152]{2,1,0:T(8,128)(2,1)} %param.28) | copy-start | bytes 2543620
  716.1 121.9 %copy-start.34 = (f32[4,1152]{1,0:T(4,128)S(1)}, f32[4,1152]{1,0:T(4,128)}, u32[]{:S(2)}) copy-start(f32[4,1152]{1,0:T(4,128)} %param.45) | copy-start | bytes 55300
  716.1 121.9 %copy-start.42 = (f32[4,1152]{1,0:T(4,128)S(1)}, f32[4,1152]{1,0:T(4,128)}, u32[]{:S(2)}) copy-start(f32[4,1152]{1,0:T(4,128)} %param.46) | copy-start | bytes 55300
  (42 other events, 1175.8 us)
Sparse Core Ops, SparseCore 0:
  15.2 31.2 all-gather.8
  49.3 51.7 all-gather.10
  103.8 37.8 all-gather.12
  146.1 26.2 reduce-scatter.16
  175.2 54.9 all-gather.16
  232.2 27.1 all-gather.14
  261.0 28.5 all-gather.20
  292.5 54.9 all-gather.18
  368.8 25.9 reduce-scatter.20
  396.9 27.4 reduce-scatter.18
  429.0 28.5 all-gather.22
  462.3 58.7 reduce-scatter.28
  525.6 77.2 reduce-scatter.30
  606.7 76.8 reduce-scatter.26
  685.8 26.2 reduce-scatter.22
  715.9 72.6 reduce-scatter.24
